TPU v7x, 32 devices: a whole 2x2x4 slice. The times are simulated.
32 devices in a mesh: shard: 2 (over x), ctx: 2 (over core), tensor: 8 (over z, y).
Axes of the slice: x: 2, y: 2, z: 4, core: 2. Of those that a mesh axis runs over, the one named last changes fastest.
Arguments:
- inputs: bfloat16 [2, 1024, 1152], P('shard', 'ctx'), may hold values from -6 to 6
- cotangent: bfloat16 [2, 1024, 1152], P('shard', 'ctx'), may hold values from -6 to 6
- attn_norm_gain: float32 [1152], replicated, may hold values from 0.1 to 1.9
- attn_norm_bias: float32 [1152], replicated, may hold values from -0.1875 to 0.1875
- qkv_weight: bfloat16 [3, 1152, 1152], P(None, 'shard', 'tensor'), may hold values from -0.8249579 to 0.8249579
- query_value_bias: float32 [2, 1152], P(None, 'tensor'), may hold values from -1.8 to 1.8
- out_weight: bfloat16 [1152, 1152], P('tensor', 'shard'), may hold values from -4 to 4
- out_bias: float32 [1152], replicated, may hold values from -1.75 to 1.75
- mlp_norm_gain: float32 [1152], replicated, may hold values from 0.1 to 1.9
- mlp_norm_bias: float32 [1152], replicated, may hold values from -1.75 to 1.75
- up_weight: bfloat16 [1152, 4304], P('shard', 'tensor'), may hold values from -0.1875 to 0.1875
- up_bias: float32 [4304], P('tensor'), may hold values from -1.75 to 1.75
- down_weight: bfloat16 [4304, 1152], P('tensor', 'shard'), may hold values from -0.1875 to 0.1875
- down_bias: float32 [1152], replicated, may hold values from -1.75 to 1.75
Outputs:
- output: bfloat16 [2, 1024, 1152], P('shard', 'ctx')
- inputs_grad: float32 [2, 1024, 1152], P('shard', 'ctx')
- attn_norm_gain_grad: float32 [1152], replicated
- attn_norm_bias_grad: float32 [1152], replicated
- qkv_weight_grad: float32 [3, 1152, 1152], P(None, 'shard', 'tensor')
- query_value_bias_grad: float32 [2, 1152], P(None, 'tensor')
- out_weight_grad: float32 [1152, 1152], P('tensor', 'shard')
- out_bias_grad: float32 [1152], replicated
- mlp_norm_gain_grad: float32 [1152], replicated
- mlp_norm_bias_grad: float32 [1152], replicated
- up_weight_grad: float32 [1152, 4304], P('shard', 'tensor')
- up_bias_grad: float32 [4304], P('tensor')
- down_weight_grad: float32 [4304, 1152], P('tensor', 'shard')
- down_bias_grad: float32 [1152], replicated
All inputs are finite; a program needn't handle non-finite values.
Results may differ from a plain program's by a relative error of at most 0.023.
Values may be sent and summed in bfloat16 or wider, within the bound.
No kernel may reach another device: no remote copies, remote signals or barrier semaphores. Data moves between devices by JAX's collectives and lax.ppermute only.
A program may use at most 128 MiB of HBM per device.

v0:
```python
import jax
import jax.numpy as jnp
from jax import lax
from jax.sharding import PartitionSpec as P

HD = 72
EPSILON = 1e-06


def layer_norm(rows, gain, shift):
    center = jnp.mean(rows, axis=-1, keepdims=True)
    offset = rows - center
    spread = jnp.mean(offset * offset, axis=-1, keepdims=True)
    return offset * lax.rsqrt(spread + EPSILON) * gain + shift


def gelu_tanh(values):
    return jax.nn.gelu(values, approximate=True)


def product(left, right):
    return jnp.dot(left, right, preferred_element_type=jnp.float32)


def split_heads(matrix):
    return matrix.reshape(matrix.shape[0], -1, HD)


def on_device(
    inputs,
    cotangent,
    attn_norm_gain,
    attn_norm_bias,
    qkv_weight,
    query_value_bias,
    out_weight,
    out_bias,
    mlp_norm_gain,
    mlp_norm_bias,
    up_weight,
    up_bias,
    down_weight,
    down_bias,
):
    rows_in = inputs[0].astype(jnp.float32)
    upstream = cotangent[0]
    upstream_f = upstream.astype(jnp.float32)
    qkv_full, out_full, up_full, down_full = (
        lax.all_gather(qkv_weight, "shard", axis=1, tiled=True),
        lax.all_gather(out_weight, "shard", axis=1, tiled=True),
        lax.all_gather(up_weight, "shard", axis=0, tiled=True),
        lax.all_gather(down_weight, "shard", axis=1, tiled=True),
    )
    scaling = HD ** (-0.5)
    normed_one, norm_one_back = jax.vjp(layer_norm, rows_in, attn_norm_gain, attn_norm_bias)
    attn_in = normed_one.astype(jnp.bfloat16)
    projected = jnp.einsum("td,cdh->cth", attn_in, qkv_full, preferred_element_type=jnp.float32)
    queries = (projected[0] + query_value_bias[0]).astype(jnp.bfloat16)
    keys_here = projected[1].astype(jnp.bfloat16)
    values_here = (projected[2] + query_value_bias[1]).astype(jnp.bfloat16)
    queries_split = split_heads(queries)
    rows_count = queries.shape[0]
    heads_local = queries_split.shape[1]
    width_local = queries.shape[1]
    run_max = jnp.full((heads_local, rows_count, 1), -jnp.inf, jnp.float32)
    run_total = jnp.zeros((heads_local, rows_count, 1), jnp.float32)
    run_accum = jnp.zeros((heads_local, rows_count, HD), jnp.float32)
    keys_block = lax.all_gather(keys_here, "ctx", axis=0, tiled=True)
    values_block = lax.all_gather(values_here, "ctx", axis=0, tiled=True)
    block_scores = (
        jnp.einsum(
            "qhd,khd->hqk",
            queries_split,
            split_heads(keys_block),
            preferred_element_type=jnp.float32,
        )
        * scaling
    )
    new_max = jnp.max(block_scores, axis=-1, keepdims=True)
    factor = jnp.exp(run_max - new_max)
    block_exp = jnp.exp(block_scores - new_max)
    new_total = run_total * factor + jnp.sum(block_exp, axis=-1, keepdims=True)
    new_accum = run_accum * factor + jnp.einsum(
        "hqk,khd->hqd",
        block_exp.astype(jnp.bfloat16),
        split_heads(values_block),
        preferred_element_type=jnp.float32,
    )
    attended = new_accum / new_total
    log_total = new_max + jnp.log(new_total)
    attended_b = (
        jnp.transpose(attended, (1, 0, 2)).reshape(rows_count, width_local).astype(jnp.bfloat16)
    )
    attn_sum = lax.psum(product(attended_b, out_full).astype(jnp.bfloat16), "tensor").astype(
        jnp.float32
    )
    residual = rows_in + attn_sum + out_bias
    normed_two, norm_two_back = jax.vjp(layer_norm, residual, mlp_norm_gain, mlp_norm_bias)
    mlp_in = normed_two.astype(jnp.bfloat16)
    hidden = product(mlp_in, up_full) + up_bias
    activ_f, gelu_back = jax.vjp(gelu_tanh, hidden)
    activated = activ_f.astype(jnp.bfloat16)
    mlp_sum = lax.psum(product(activated, down_full).astype(jnp.bfloat16), "tensor").astype(
        jnp.float32
    )
    output = (residual + mlp_sum + down_bias).astype(jnp.bfloat16)
    down_bias_grad = jnp.sum(upstream_f, axis=0)
    down_grad = jnp.einsum("tf,td->fd", activated, upstream, preferred_element_type=jnp.float32)
    d_activated = jnp.einsum("td,fd->tf", upstream, down_full, preferred_element_type=jnp.float32)
    (d_hidden,) = gelu_back(d_activated)
    up_bias_grad = jnp.sum(d_hidden, axis=0)
    d_hidden_b = d_hidden.astype(jnp.bfloat16)
    up_grad = jnp.einsum("td,tf->df", mlp_in, d_hidden_b, preferred_element_type=jnp.float32)
    d_mlp_part = jnp.einsum("tf,df->td", d_hidden_b, up_full, preferred_element_type=jnp.float32)
    d_mlp_in = lax.psum(d_mlp_part.astype(jnp.bfloat16), "tensor").astype(jnp.float32)
    d_norm_two, mlp_gain_grad, mlp_shift_grad = norm_two_back(d_mlp_in)
    d_residual = upstream_f + d_norm_two
    out_bias_grad = jnp.sum(d_residual, axis=0)
    d_residual_b = d_residual.astype(jnp.bfloat16)
    out_grad = jnp.einsum("th,td->hd", attended_b, d_residual_b, preferred_element_type=jnp.float32)
    d_attended = jnp.einsum(
        "td,hd->th", d_residual_b, out_full, preferred_element_type=jnp.float32
    ).astype(jnp.bfloat16)
    d_attended_split = split_heads(d_attended)
    delta = jnp.sum(
        d_attended_split.astype(jnp.float32) * split_heads(attended_b).astype(jnp.float32), axis=-1
    )
    delta = jnp.transpose(delta)[:, :, None]
    keys_back, values_back = (
        lax.all_gather(keys_here, "ctx", axis=0, tiled=True),
        lax.all_gather(values_here, "ctx", axis=0, tiled=True),
    )
    keys_split = split_heads(keys_back)
    values_split = split_heads(values_back)
    scores_back = (
        jnp.einsum("qhd,khd->hqk", queries_split, keys_split, preferred_element_type=jnp.float32)
        * scaling
    )
    probs = jnp.exp(scores_back - log_total)
    d_probs = jnp.einsum(
        "qhd,khd->hqk", d_attended_split, values_split, preferred_element_type=jnp.float32
    )
    d_scores_b = (probs * (d_probs - delta)).astype(jnp.bfloat16)
    probs_b = probs.astype(jnp.bfloat16)
    d_queries = (
        jnp.einsum("hqk,khd->qhd", d_scores_b, keys_split, preferred_element_type=jnp.float32)
        * scaling
    ).reshape(rows_count, width_local)
    key_terms = (
        jnp.einsum("hqk,qhd->khd", d_scores_b, queries_split, preferred_element_type=jnp.float32)
        * scaling
    ).reshape(-1, width_local)
    value_terms = jnp.einsum(
        "hqk,qhd->khd", probs_b, d_attended_split, preferred_element_type=jnp.float32
    ).reshape(-1, width_local)
    kv_grad = lax.psum_scatter(
        jnp.concatenate([key_terms, value_terms], axis=1).astype(jnp.bfloat16),
        "ctx",
        scatter_dimension=0,
        tiled=True,
    ).astype(jnp.float32)
    d_keys = kv_grad[:, :width_local]
    d_values = kv_grad[:, width_local:]
    bias_grad = jnp.stack([jnp.sum(d_queries, axis=0), jnp.sum(d_values, axis=0)])
    d_proj = jnp.stack([d_queries, d_keys, d_values]).astype(jnp.bfloat16)
    qkv_grad = jnp.einsum("td,cth->cdh", attn_in, d_proj, preferred_element_type=jnp.float32)
    d_attn_part = jnp.einsum("cth,cdh->td", d_proj, qkv_full, preferred_element_type=jnp.float32)
    d_attn_in = lax.psum(d_attn_part.astype(jnp.bfloat16), "tensor").astype(jnp.float32)
    d_norm_one, attn_gain_grad, attn_shift_grad = norm_one_back(d_attn_in)
    inputs_grad = d_residual + d_norm_one
    matrices = (qkv_grad, out_grad, up_grad, down_grad)
    summed = (
        lax.psum(matrices[0].astype(jnp.bfloat16), "ctx").astype(jnp.float32),
        lax.psum(matrices[1].astype(jnp.bfloat16), "ctx").astype(jnp.float32),
        lax.psum(matrices[2].astype(jnp.bfloat16), "ctx").astype(jnp.float32),
        lax.psum(matrices[3].astype(jnp.bfloat16), "ctx").astype(jnp.float32),
    )
    owned = (
        lax.psum_scatter(
            summed[0].astype(jnp.bfloat16), "shard", scatter_dimension=1, tiled=True
        ).astype(jnp.float32),
        lax.psum_scatter(
            summed[1].astype(jnp.bfloat16), "shard", scatter_dimension=1, tiled=True
        ).astype(jnp.float32),
        lax.psum_scatter(
            summed[2].astype(jnp.bfloat16), "shard", scatter_dimension=0, tiled=True
        ).astype(jnp.float32),
        lax.psum_scatter(
            summed[3].astype(jnp.bfloat16), "shard", scatter_dimension=1, tiled=True
        ).astype(jnp.float32),
    )
    vectors = lax.psum(
        (
            attn_gain_grad,
            attn_shift_grad,
            bias_grad,
            out_bias_grad,
            mlp_gain_grad,
            mlp_shift_grad,
            up_bias_grad,
            down_bias_grad,
        ),
        ("shard", "ctx"),
    )
    return (
        output[None],
        inputs_grad[None],
        vectors[0],
        vectors[1],
        owned[0],
        vectors[2],
        owned[1],
        vectors[3],
        vectors[4],
        vectors[5],
        owned[2],
        vectors[6],
        owned[3],
        vectors[7],
    )


def solution(mesh):
    in_specs = (
        P("shard", "ctx", None),
        P("shard", "ctx", None),
        P(),
        P(),
        P(None, "shard", "tensor"),
        P(None, "tensor"),
        P("tensor", "shard"),
        P(),
        P(),
        P(),
        P("shard", "tensor"),
        P("tensor"),
        P("tensor", "shard"),
        P(),
    )
    out_specs = (
        P("shard", "ctx", None),
        P("shard", "ctx", None),
        P(),
        P(),
        P(None, "shard", "tensor"),
        P(None, "tensor"),
        P("tensor", "shard"),
        P(),
        P(),
        P(),
        P("shard", "tensor"),
        P("tensor"),
        P("tensor", "shard"),
        P(),
    )
    return jax.shard_map(
        on_device, mesh=mesh, in_specs=in_specs, out_specs=out_specs, check_vma=False
    )
```

profile of v0, /device:TPU:0, one launch (start us, length us, event | category | flops | bytes accessed | tf_op | source)
XLA Modules:
  0.0 525.6 jit_solution(9866181186982959166)
XLA Ops:
  12.6 29.7 %all_gather.20 = bf16[3,1152,144]{2,0,1:T(4,128)(2,1)} all-gather(bf16[3,576,144]{2,0,1:T(4,128)(2,1)S(1)} %copy.31), channel_id=1, replica_groups=mesh['shard'=2,'ctx'=2,'tensor'=8] {'shard'}, dimensions={1}, use_global_device_ids=true | all-gather | bytes 1492992 | tf_op jit(solution)/shard_map/all_gather | solution.py:49
  42.3 4.0 copy.32
  52.4 7.3 %all-gather.1 = bf16[2,576,144]{1,2,0:T(8,128)(2,1)S(1)} all-gather(bf16[1,576,144]{1,2,0:T(8,128)(2,1)S(1)} %bitcast.203), channel_id=1, replica_groups=mesh['shard'=2,'ctx'=2,'tensor'=8] {'shard'}, dimensions={0}, use_global_device_ids=true | all-gather | bytes 497664 | tf_op jit(solution)/shard_map/all_gather | solution.py:50
  63.4 3.2 fusion.51
  69.7 80.4 %all-reduce.8.cloned.1.call-done = bf16[512,1152]{1,0:T(8,128)(2,1)} async-done(((bf16[512,1152]{1,0:T(8,128)(2,1)}), bf16[512,1152]{1,0:T(8,128)(2,1)}) %all-reduce.8.cloned.1.call-update) | async-done | bytes 1179664 | tf_op jit(solution)/shard_map/psum | solution.py:94
  152.6 3.5 copy.34
  156.1 4.0 reshape.163
  160.1 3.5 copy.35
  163.6 4.1 reshape.165
  175.9 79.3 %all-reduce.10.cloned.1.call-done = bf16[512,1152]{1,0:T(8,128)(2,1)} async-done(((bf16[512,1152]{1,0:T(8,128)(2,1)}), bf16[512,1152]{1,0:T(8,128)(2,1)}) %all-reduce.10.cloned.1.call-update) | async-done | bytes 1179664 | tf_op jit(solution)/shard_map/psum | solution.py:115
  255.2 2.9 convert_reduce_fusion.1
  272.6 3.7 convolution_convert_fusion
  279.0 3.3 convolution_convert_fusion.1
  290.3 3.3 copy.37
  293.6 5.4 %reshape.170 = bf16[1152,432]{1,0:T(8,128)(2,1)} reshape(bf16[1152,3,144]{2,1,0:T(4,128)(2,1)} %bitcast.178) | data formatting | bytes 1990656
  299.3 4.0 convolution_convert_fusion.4
  307.8 14.7 %reduce-scatter.22.cloned.1.call-done = bf16[576,538]{1,0:T(8,128)(2,1)} async-done(((bf16[1152,538]{1,0:T(8,128)(2,1)}), bf16[576,538]{1,0:T(8,128)(2,1)}) %reduce-scatter.22.cloned.1.call-update) | async-done | bytes 619792
  324.8 24.9 %reduce-scatter.20.cloned.1.call-done = bf16[576,538]{1,0:T(8,128)(2,1)} async-done(((bf16[1152,538]{1,0:T(8,128)(2,1)}), bf16[576,538]{1,0:T(8,128)(2,1)}) %reduce-scatter.20.cloned.1.call-update) | async-done | bytes 619792
  352.0 22.4 %reduce-scatter.16.cloned.1.call-done = bf16[576,432]{1,0:T(8,128)(2,1)} async-done(((bf16[1152,432]{1,0:T(8,128)(2,1)}), bf16[576,432]{1,0:T(8,128)(2,1)}) %reduce-scatter.16.cloned.1.call-update) | async-done | bytes 497680
  374.4 2.9 reshape.171
  379.4 108.3 %all-reduce.12.cloned.1.call-done = (bf16[512,1152]{1,0:T(8,128)(2,1)}, bf16[512,1152]{1,0:T(8,128)(2,1)}) async-done(((bf16[512,1152]{1,0:T(8,128)(2,1)}, bf16[512,1152]{1,0:T(8,128)(2,1)}), (bf16[512,1152]{1,0:T(8,128)(2,1)}, bf16[512,1152]{1,0:T(8,128)(2,1)})) %all-reduce.12.cloned.1.call-update) | async-done | bytes 2359312 | tf_op jit(solution)/shard_map/psum | solution.py:103
  492.3 11.9 %all-reduce = (f32[1152]{0:T(1024)}, f32[1152]{0:T(1024)}, f32[2,144]{1,0:T(2,128)}, f32[1152]{0:T(1024)}, f32[1152]{0:T(1024)}, /*index=5*/f32[1152]{0:T(1024)}, f32[538]{0:T(1024)}, f32[1152]{0:T(1024)}) all-reduce(f32[1152]{0:T(1024)} %get-tuple-element.16, ...), channel_id=1, replica_groups=mesh['shard'=2,'ctx'=2,'tensor'=8] {'shard','ctx'}, use_global_device_ids=true, to_apply=%region_17.0 | all-reduce | flops 7738 | bytes 61904 | tf_op jit(solution)/shard_map/psum | solution.py:192
  504.8 4.2 add_bitcast_fusion
  509.0 3.1 all-reduce.14.cloned.1.call-done
  (172 shorter events, 75.7 us)
Async XLA Ops:
  8.0 142.1 %all-reduce.8.cloned.1.call-start = ((), (), s32[]{:S(2)}) async-start(), calls=%async_computation.5 | async-start | bytes 2359296 | tf_op jit(solution)/shard_map/psum | solution.py:94
  9.6 279.0 %copy-start.29 = (f32[512]{0:T(512)}, f32[512]{0:T(512)S(1)}, u32[]{:S(2)}) copy-start(f32[512]{0:T(512)S(1)} %broadcast_multiply_fusion.1) | copy-start | bytes 6148
  11.4 277.3 %copy-start.34 = (f32[512]{0:T(512)}, f32[512]{0:T(512)S(1)}, u32[]{:S(2)}) copy-start(f32[512]{0:T(512)S(1)} %fusion.70) | copy-start | bytes 6148
  42.3 4.0 copy-start.28
  42.3 4.0 copy-start.38
  51.3 8.5 %copy-start.1 = (f32[2,512,1024]{2,1,0:T(8,128)}, f32[2,512,1024]{2,1,0:T(8,128)S(1)}, u32[]{:S(2)}) copy-start(f32[2,512,1024]{2,1,0:T(8,128)S(1)} %get-tuple-element.50) | copy-start | bytes 12582916
  66.6 83.4 %copy-start.21 = (f32[1152]{0:T(1024)S(1)}, f32[1152]{0:T(1024)}, u32[]{:S(2)}) copy-start(f32[1152]{0:T(1024)} %param.21) | copy-start | bytes 13828
  68.3 84.3 %all-gather.7.cloned.1.call-start = ((), (), s32[]{:S(2)}) async-start(), calls=%async_computation.8 | async-start | bytes 2088960 | tf_op jit(solution)/shard_map/all_gather | solution.py:51
  68.8 91.3 %all-gather.9.cloned.1.call-start = ((), (), s32[]{:S(2)}) async-start(), calls=%async_computation.9 | async-start | bytes 2088960 | tf_op jit(solution)/shard_map/all_gather | solution.py:52
  69.4 185.8 %all-reduce.10.cloned.1.call-start = ((), (), s32[]{:S(2)}) async-start(), calls=%async_computation.6 | async-start | bytes 2359296 | tf_op jit(solution)/shard_map/psum | solution.py:115
  160.1 7.6 %copy-start.27 = (f32[1152]{0:T(1024)S(1)}, f32[1152]{0:T(1024)}, u32[]{:S(2)}) copy-start(f32[1152]{0:T(1024)} %param.22) | copy-start | bytes 13828
  160.1 7.6 %copy-start.37 = (f32[1152]{0:T(1024)S(1)}, f32[1152]{0:T(1024)}, u32[]{:S(2)}) copy-start(f32[1152]{0:T(1024)} %param.23) | copy-start | bytes 13828
  160.1 7.6 %copy-start.40 = (f32[538]{0:T(1024)S(1)}, f32[538]{0:T(1024)}, u32[]{:S(2)}) copy-start(f32[538]{0:T(1024)} %param.25) | copy-start | bytes 6460
  175.6 112.0 %reduce-scatter.14.cloned.1.call-start = ((), (), s32[]{:S(2)}) async-start(), calls=%async_computation.7 | async-start | bytes 884736 | tf_op jit(solution)/shard_map/reduce_scatter | solution.py:156
  260.1 4.2 copy-start.2
  269.4 36.0 %reduce-scatter.18.cloned.1.call-start = ((), (), s32[]{:S(2)}) async-start(), calls=%async_computation.11 | async-start | bytes 884736
  272.6 49.9 %reduce-scatter.22.cloned.1.call-start = ((), (), s32[]{:S(2)}) async-start(), calls=%async_computation.13 | async-start | bytes 2211840
  279.0 70.7 %reduce-scatter.20.cloned.1.call-start = ((), (), s32[]{:S(2)}) async-start(), calls=%async_computation.12 | async-start | bytes 2211840
  284.8 4.5 copy-start.39
  284.9 89.5 %reduce-scatter.16.cloned.1.call-start = ((), (), s32[]{:S(2)}) async-start(), calls=%async_computation.10 | async-start | bytes 1769472
  299.0 4.3 copy-start.15
  299.0 188.7 %all-reduce.12.cloned.1.call-start = ((), (), s32[]{:S(2)}) async-start(), calls=%async_computation.14 | async-start | bytes 4718592 | tf_op jit(solution)/shard_map/psum | solution.py:103
  305.2 207.0 %all-reduce.14.cloned.1.call-start = ((), (), s32[]{:S(2)}) async-start(), calls=%async_computation.15 | async-start | bytes 4259840 | tf_op jit(solution)/shard_map/psum | solution.py:173
  512.2 5.1 copy-start.16
  (30 other events, 66.5 us)
Sparse Core Ops, SparseCore 0:
  68.4 81.6 all-reduce.7
  175.7 79.4 all-reduce.9
  269.5 7.1 reduce-scatter.13
  278.8 16.4 reduce-scatter.17
  297.4 25.0 reduce-scatter.21
  324.6 25.0 reduce-scatter.19
  352.5 21.8 reduce-scatter.15
  379.1 108.5 all-reduce.11
  491.4 20.6 all-reduce.13
Sparse Core Ops, SparseCore 1:
  70.3 26.5 all-gather.6
  98.3 25.0 all-gather.8
where the time goes:
time: 527 us; the launch traced here: 526 us
  waiting for transfers between devices  334 us (63%)
  local copies, waits for them, and re-layouts  53.7 us (10%)
  blocking collectives  52.9 us (10%)
  matrix products  35.4 us (7%)
  other arithmetic  32.1 us (6%)
  between operations  15.8 us (3%)
    psum x1, waiting for transfers between devices, on_device(): lax.psum(product(activated, down_full).astype(jnp.bfloat16), 'tensor')  108 us
    psum x1, waiting for transfers between devices, on_device(): lax.psum(product(attended_b, out_full).astype(jnp.bfloat16), 'tensor')  80.4 us
    psum x1, waiting for transfers between devices, on_device(): lax.psum(d_mlp_part.astype(jnp.bfloat16), 'tensor').astype(jnp.float32)  79.3 us
    unnamed x15, waiting for transfers between devices  63.2 us
    unnamed x100, local copies, waits for them, and re-layouts  41.2 us
    all_gather x1, blocking collectives, on_device(): lax.all_gather(qkv_weight, 'shard', axis=1, tiled=True)  29.7 us
    psum x1, blocking collectives, on_device(): lax.psum((attn_gain_grad, attn_shift_grad, bias_grad, out_bias_grad, mlp_...  11.9 us
  transfers between devices with their start and end apart: 11, of which 7 were waited for; matrix products, arithmetic and copies ran while one was open for 13% of the time, Pallas kernels for 0%

commit v1 on v0

--- a/solution.py
+++ b/solution.py
@@ -5,6 +5,29 @@
 
 HD = 72
 EPSILON = 1e-06
+
+
+def in_order(parts, dim):
+    lengths = list(parts.shape[1:])
+    lengths[dim] *= parts.shape[0]
+    return jnp.moveaxis(parts, 0, dim).reshape(lengths)
+
+
+def collected_by_bits(value, axis):
+    size, mine = (lax.axis_size(axis), lax.axis_index(axis))
+    pieces, bit = (value[None], 1)
+    while bit < size:
+        received = lax.ppermute(pieces, axis, [(i, i ^ bit) for i in range(size)])
+        low = mine & bit == 0
+        pieces = jnp.concatenate(
+            [jnp.where(low, pieces, received), jnp.where(low, received, pieces)]
+        )
+        bit *= 2
+    return pieces
+
+
+def doubled_up(x, axis, dim):
+    return in_order(collected_by_bits(x, axis), dim)
 
 
 def layer_norm(rows, gain, shift):
@@ -46,7 +69,7 @@
     upstream = cotangent[0]
     upstream_f = upstream.astype(jnp.float32)
     qkv_full, out_full, up_full, down_full = (
-        lax.all_gather(qkv_weight, "shard", axis=1, tiled=True),
+        doubled_up(qkv_weight, "shard", 1),
         lax.all_gather(out_weight, "shard", axis=1, tiled=True),
         lax.all_gather(up_weight, "shard", axis=0, tiled=True),
         lax.all_gather(down_weight, "shard", axis=1, tiled=True),

time: 527 us -> 497 us (0.943); the launches traced: 526 us -> 490 us
  waiting for transfers between devices: 334 us -> 319 us
  blocking collectives: 52.9 us -> 38 us
    all_gather x1 -> x0, blocking collectives: 29.7 us -> none  [on_device(): lax.all_gather(qkv_weight, 'shard', axis=1, tiled=True)]
    psum x1, waiting for transfers between devices: 80.4 us -> 51.8 us  [on_device(): lax.psum(product(attended_b, out_full).astype(jnp.bfloat16), 'tensor')]
    all_gather x1, blocking collectives: 7.34 us -> 22.1 us  [on_device(): lax.all_gather(out_weight, 'shard', axis=1, tiled=True)]
    all_gather x1, waiting for transfers between devices: 0.02 us -> 14.5 us  [on_device(): lax.all_gather(down_weight, 'shard', axis=1, tiled=True)]
    unnamed x100 -> x99, local copies, waits for them, and re-layouts: 41.2 us -> 40.3 us
  transfers between devices with their start and end apart: 11 -> 12, of which waited for: 7 -> 8; matrix products, arithmetic and copies ran while one was open for 13% -> 17% of each run, Pallas kernels for 0% -> 0%
where the time goes in v1:
time: 497 us; the launch traced here: 490 us
  waiting for transfers between devices  319 us (64%)
  local copies, waits for them, and re-layouts  50.4 us (10%)
  blocking collectives  38 us (8%)
  matrix products  31.7 us (6%)
  other arithmetic  30.2 us (6%)
  between operations  16.6 us (3%)
    psum x1, waiting for transfers between devices, on_device(): lax.psum(product(activated, down_full).astype(jnp.bfloat16), 'tensor')  108 us
    psum x1, waiting for transfers between devices, on_device(): lax.psum(d_mlp_part.astype(jnp.bfloat16), 'tensor').astype(jnp.float32)  78.8 us
    unnamed x15, waiting for transfers between devices  62.9 us
    psum x1, waiting for transfers between devices, on_device(): lax.psum(product(attended_b, out_full).astype(jnp.bfloat16), 'tensor')  51.8 us
    unnamed x99, local copies, waits for them, and re-layouts  40.3 us
    all_gather x1, blocking collectives, on_device(): lax.all_gather(out_weight, 'shard', axis=1, tiled=True)  22.1 us
    all_gather x1, waiting for transfers between devices, on_device(): lax.all_gather(down_weight, 'shard', axis=1, tiled=True)  14.5 us
    psum x1, blocking collectives, on_device(): lax.psum((attn_gain_grad, attn_shift_grad, bias_grad, out_bias_grad, mlp_...  11.9 us
  transfers between devices with their start and end apart: 12, of which 8 were waited for; matrix products, arithmetic and copies ran while one was open for 17% of the time, Pallas kernels for 0%

profile of v1, /device:TPU:0, one launch (start us, length us, event | category | flops | bytes accessed | tf_op | source)
XLA Modules:
  0.0 490.0 jit_solution(12188898102924258061)
XLA Ops:
  8.8 3.0 collective-permute-start
  13.6 22.1 %all-gather.1 = bf16[2,576,144]{1,2,0:T(8,128)(2,1)S(1)} all-gather(bf16[1,576,144]{1,2,0:T(8,128)(2,1)S(1)} %bitcast.206), channel_id=1, replica_groups=mesh['shard'=2,'ctx'=2,'tensor'=8] {'shard'}, dimensions={0}, use_global_device_ids=true | all-gather | bytes 497664 | tf_op jit(solution)/shard_map/all_gather | solution.py:73
  49.8 3.5 copy.35
  53.3 4.1 reshape.194
  57.4 14.5 %all-gather.9.cloned.1.call-done = bf16[2,576,538]{1,2,0:T(8,128)(2,1)} async-done(((bf16[1,576,538]{1,2,0:T(8,128)(2,1)}), bf16[2,576,538]{1,2,0:T(8,128)(2,1)}) %all-gather.9.cloned.1.call-update) | async-done | bytes 1239568 | tf_op jit(solution)/shard_map/all_gather | solution.py:75
  72.0 3.5 copy.36
  75.4 4.1 reshape.196
  79.5 51.8 %all-reduce.8.cloned.1.call-done = bf16[512,1152]{1,0:T(8,128)(2,1)} async-done(((bf16[512,1152]{1,0:T(8,128)(2,1)}), bf16[512,1152]{1,0:T(8,128)(2,1)}) %all-reduce.8.cloned.1.call-update) | async-done | bytes 1179664 | tf_op jit(solution)/shard_map/psum | solution.py:117
  141.0 78.8 %all-reduce.10.cloned.1.call-done = bf16[512,1152]{1,0:T(8,128)(2,1)} async-done(((bf16[512,1152]{1,0:T(8,128)(2,1)}), bf16[512,1152]{1,0:T(8,128)(2,1)}) %all-reduce.10.cloned.1.call-update) | async-done | bytes 1179664 | tf_op jit(solution)/shard_map/psum | solution.py:138
  219.8 2.9 convert_reduce_fusion.1
  237.3 3.7 convolution_convert_fusion
  243.6 3.3 convolution_convert_fusion.1
  254.9 3.3 copy.37
  258.2 5.4 %reshape.200 = bf16[1152,432]{1,0:T(8,128)(2,1)} reshape(bf16[1152,3,144]{2,1,0:T(4,128)(2,1)} %bitcast.184) | data formatting | bytes 1990656
  263.9 4.0 convolution_convert_fusion.4
  272.4 14.8 %reduce-scatter.22.cloned.1.call-done = bf16[576,538]{1,0:T(8,128)(2,1)} async-done(((bf16[1152,538]{1,0:T(8,128)(2,1)}), bf16[576,538]{1,0:T(8,128)(2,1)}) %reduce-scatter.22.cloned.1.call-update) | async-done | bytes 619792
  289.5 25.0 %reduce-scatter.20.cloned.1.call-done = bf16[576,538]{1,0:T(8,128)(2,1)} async-done(((bf16[1152,538]{1,0:T(8,128)(2,1)}), bf16[576,538]{1,0:T(8,128)(2,1)}) %reduce-scatter.20.cloned.1.call-update) | async-done | bytes 619792
  316.8 22.2 %reduce-scatter.16.cloned.1.call-done = bf16[576,432]{1,0:T(8,128)(2,1)} async-done(((bf16[1152,432]{1,0:T(8,128)(2,1)}), bf16[576,432]{1,0:T(8,128)(2,1)}) %reduce-scatter.16.cloned.1.call-update) | async-done | bytes 497680
  339.0 2.9 reshape.201
  344.0 107.8 %all-reduce.12.cloned.1.call-done = (bf16[512,1152]{1,0:T(8,128)(2,1)}, bf16[512,1152]{1,0:T(8,128)(2,1)}) async-done(((bf16[512,1152]{1,0:T(8,128)(2,1)}, bf16[512,1152]{1,0:T(8,128)(2,1)}), (bf16[512,1152]{1,0:T(8,128)(2,1)}, bf16[512,1152]{1,0:T(8,128)(2,1)})) %all-reduce.12.cloned.1.call-update) | async-done | bytes 2359312 | tf_op jit(solution)/shard_map/psum | solution.py:126
  451.9 2.7 convert_reduce_fusion
  456.4 11.9 %all-reduce = (f32[1152]{0:T(1024)}, f32[1152]{0:T(1024)}, f32[2,144]{1,0:T(2,128)}, f32[1152]{0:T(1024)}, f32[1152]{0:T(1024)}, /*index=5*/f32[1152]{0:T(1024)}, f32[538]{0:T(1024)}, f32[1152]{0:T(1024)}) all-reduce(f32[1152]{0:T(1024)} %get-tuple-element.16, ...), channel_id=1, replica_groups=mesh['shard'=2,'ctx'=2,'tensor'=8] {'shard','ctx'}, use_global_device_ids=true, to_apply=%region_17.18 | all-reduce | flops 7738 | bytes 61904 | tf_op jit(solution)/shard_map/psum | solution.py:215
  469.0 4.2 add_bitcast_fusion
  473.2 2.7 all-reduce.14.cloned.1.call-done
  (175 shorter events, 71.2 us)
Async XLA Ops:
  8.0 29.0 %copy-start = (bf16[1,512,1152]{2,1,0:T(8,128)(2,1)S(1)}, bf16[1,512,1152]{2,1,0:T(8,128)(2,1)}, u32[]{:S(2)}) copy-start(bf16[1,512,1152]{2,1,0:T(8,128)(2,1)} %param.14) | copy-start | bytes 3538948
  8.0 5.5 %copy-start.36 = (f32[2,144]{1,0:T(2,128)S(1)}, f32[2,144]{1,0:T(2,128)}, u32[]{:S(2)}) copy-start(f32[2,144]{1,0:T(2,128)} %param.19) | copy-start | bytes 3460
  8.0 5.6 %copy-start.22 = (bf16[144,576]{1,0:T(8,128)(2,1)S(1)}, bf16[144,576]{1,0:T(8,128)(2,1)}, u32[]{:S(2)}) copy-start(bf16[144,576]{1,0:T(8,128)(2,1)} %param.20) | copy-start | bytes 497668
  8.0 41.8 %all-gather.7.cloned.1.call-start = ((), (), s32[]{:S(2)}) async-start(), calls=%async_computation.8 | async-start | bytes 2088960 | tf_op jit(solution)/shard_map/all_gather | solution.py:74
  8.8 63.2 %all-gather.9.cloned.1.call-start = ((), (), s32[]{:S(2)}) async-start(), calls=%async_computation.9 | async-start | bytes 2088960 | tf_op jit(solution)/shard_map/all_gather | solution.py:75
  8.8 28.7 %collective-permute-start = (bf16[1,3,576,144]{2,3,1,0:T(8,128)(2,1)}, bf16[1,3,576,144]{2,3,1,0:T(8,128)(2,1)S(1)}, u32[]{:S(2)}, u32[]{:S(2)}) collective-permute-start(bf16[1,3,576,144]{2,3,1,0:T(8,128)(2,1)} %bitcast.204), channel_id=1, source_target_pairs={{0,16},{16,0},{1,17},{17,1},{2,18},{18,2},{3,19},{19,3},{4,20},{20... | collective-permute-start | bytes 1493000 | tf_op jit(solution)/shard_map/ppermute | solution.py:20
  11.9 25.6 %copy-start.20 = (bf16[3,576,144]{1,2,0:T(8,128)(2,1)S(1)}, bf16[3,576,144]{1,2,0:T(8,128)(2,1)}, u32[]{:S(2)}) copy-start(bf16[3,576,144]{1,2,0:T(8,128)(2,1)} %param.18) | copy-start | bytes 1492996
  11.9 119.4 %all-reduce.8.cloned.1.call-start = ((), (), s32[]{:S(2)}) async-start(), calls=%async_computation.5 | async-start | bytes 2359296 | tf_op jit(solution)/shard_map/psum | solution.py:117
  13.5 239.8 %copy-start.29 = (f32[512]{0:T(512)}, f32[512]{0:T(512)S(1)}, u32[]{:S(2)}) copy-start(f32[512]{0:T(512)S(1)} %broadcast_multiply_fusion.1) | copy-start | bytes 6148
  37.5 215.8 %copy-start.34 = (f32[512]{0:T(512)}, f32[512]{0:T(512)S(1)}, u32[]{:S(2)}) copy-start(f32[512]{0:T(512)S(1)} %fusion.85) | copy-start | bytes 6148
  49.3 170.6 %all-reduce.10.cloned.1.call-start = ((), (), s32[]{:S(2)}) async-start(), calls=%async_computation.6 | async-start | bytes 2359296 | tf_op jit(solution)/shard_map/psum | solution.py:138
  57.4 73.9 %copy-start.21 = (f32[1152]{0:T(1024)S(1)}, f32[1152]{0:T(1024)}, u32[]{:S(2)}) copy-start(f32[1152]{0:T(1024)} %param.21) | copy-start | bytes 13828
  79.5 54.3 %copy-start.27 = (f32[1152]{0:T(1024)S(1)}, f32[1152]{0:T(1024)}, u32[]{:S(2)}) copy-start(f32[1152]{0:T(1024)} %param.22) | copy-start | bytes 13828
  79.5 54.4 %copy-start.37 = (f32[1152]{0:T(1024)S(1)}, f32[1152]{0:T(1024)}, u32[]{:S(2)}) copy-start(f32[1152]{0:T(1024)} %param.23) | copy-start | bytes 13828
  79.5 54.4 %copy-start.40 = (f32[538]{0:T(1024)S(1)}, f32[538]{0:T(1024)}, u32[]{:S(2)}) copy-start(f32[538]{0:T(1024)} %param.25) | copy-start | bytes 6460
  140.8 111.4 %reduce-scatter.14.cloned.1.call-start = ((), (), s32[]{:S(2)}) async-start(), calls=%async_computation.7 | async-start | bytes 884736 | tf_op jit(solution)/shard_map/reduce_scatter | solution.py:179
  234.0 35.9 %reduce-scatter.18.cloned.1.call-start = ((), (), s32[]{:S(2)}) async-start(), calls=%async_computation.11 | async-start | bytes 884736
  237.2 50.0 %reduce-scatter.22.cloned.1.call-start = ((), (), s32[]{:S(2)}) async-start(), calls=%async_computation.13 | async-start | bytes 2211840
  243.6 70.9 %reduce-scatter.20.cloned.1.call-start = ((), (), s32[]{:S(2)}) async-start(), calls=%async_computation.12 | async-start | bytes 2211840
  249.5 4.5 copy-start.39
  249.5 89.5 %reduce-scatter.16.cloned.1.call-start = ((), (), s32[]{:S(2)}) async-start(), calls=%async_computation.10 | async-start | bytes 1769472
  263.6 188.3 %all-reduce.12.cloned.1.call-start = ((), (), s32[]{:S(2)}) async-start(), calls=%async_computation.14 | async-start | bytes 4718592 | tf_op jit(solution)/shard_map/psum | solution.py:126
  269.8 206.1 %all-reduce.14.cloned.1.call-start = ((), (), s32[]{:S(2)}) async-start(), calls=%async_computation.15 | async-start | bytes 4259840 | tf_op jit(solution)/shard_map/psum | solution.py:196
  475.9 5.1 %copy-start.17 = (bf16[538,576]{1,0:T(8,128)(2,1)S(1)}, bf16[538,576]{1,0:T(8,128)(2,1)}, u32[]{:S(2)}) copy-start(bf16[538,576]{1,0:T(8,128)(2,1)} %get-tuple-element.35) | copy-start | bytes 1859332
  (31 other events, 66.2 us)
Sparse Core Ops, SparseCore 0:
  10.4 33.2 all-gather.6
  45.3 26.6 all-gather.8
Sparse Core Ops, SparseCore 1:
  49.4 81.9 all-reduce.7
  140.9 78.9 all-reduce.9
  234.1 7.1 reduce-scatter.13
  243.5 16.3 reduce-scatter.17
  262.2 25.0 reduce-scatter.21
  289.5 25.0 reduce-scatter.19
  317.2 21.7 reduce-scatter.15
  343.6 108.2 all-reduce.11
  455.4 20.4 all-reduce.13
